TPU v7x, 128 devices: a whole 4x4x4 slice. The times are simulated.
128 devices in a mesh: path: 4 (over z_lo, core), ctx: 32 (over x, z_hi, y).
Axes of the slice: x: 4, y: 4, z: 4 (z_hi: 2, z_lo: 2; z = z_hi * 2 + z_lo), core: 2. Of those that a mesh axis runs over, the one named last changes fastest.
Arguments:
- tokens: int32 [4096], P('ctx'), may hold values from 0 to 511
- sub_pos: int32 [512], P('ctx'), may hold values from 0 to 4095, as said below
- sub_base: int32 [512], P('ctx'), may hold values from 0 to 511
- embed: bfloat16 [512, 4096], replicated, may hold values from -6 to 6
- norm_gain: float32 [4096], replicated, may hold values from 0.1 to 1.9
- fir_taps: bfloat16 [3, 3, 4096], replicated, may hold values from -3.5 to 3.5
- long_filter: float32 [4096, 4096], P(None, 'ctx'), may hold values from -8 to 8
- skip_gain: float32 [4096], P('ctx'), may hold values from 0.5 to 1.5
- cotangent: bfloat16 [4096, 4096], P('ctx'), may hold values from -6 to 6
Outputs:
- path_grad: float32 [4096, 4096], P('ctx', 'path')
- attribution: float32 [4096, 4096], P('ctx', 'path')
Inputs may be any that keep to these rules, and one draw needn't show every extreme that they name: `sub_pos`: exactly one substituted position in each aligned block of 8 tokens, so the positions rise strictly.
All inputs are finite; a program needn't handle non-finite values.
Results may differ from a plain program's by a relative error of at most 0.0085.
Values may be sent and summed in bfloat16 or wider, within the bound.
A program may use at most 192 MiB of HBM per device.

v0:
```python
import jax
import jax.numpy as jnp
from jax import lax
from jax.sharding import PartitionSpec as P

PATH_DEV = 1
precise = lax.Precision.HIGH


def from_behind(block, axis, distance):
    devices = range(lax.axis_size(axis))
    route = [(i - distance, i) for i in devices if i - distance in devices]
    return lax.ppermute(block, axis, route)


def angle_tables(length):
    outer_size = 64
    inner_size = length // outer_size
    outer_idx = jnp.arange(outer_size, dtype=jnp.int32)
    inner_idx = jnp.arange(inner_size, dtype=jnp.int32)
    outer_angle = (
        2.0
        * jnp.pi
        / outer_size
        * (outer_idx[:, None] * outer_idx[None, :] % outer_size).astype(jnp.float32)
    )
    inner_angle = (
        2.0
        * jnp.pi
        / inner_size
        * (inner_idx[:, None] * inner_idx[None, :] % inner_size).astype(jnp.float32)
    )
    twist_angle = (
        2.0
        * jnp.pi
        / length
        * (outer_idx[:, None] * inner_idx[None, :] % length).astype(jnp.float32)
    )
    return (outer_angle, inner_angle, twist_angle)


def complex_table(angle, sign):
    cosine = jnp.cos(angle)
    sine = sign * jnp.sin(angle)
    return jnp.stack([jnp.stack([cosine, sine]), jnp.stack([-sine, cosine])])


def twisted(values, angle, sign):
    cosine = jnp.cos(angle)[None, :, :, None]
    sine = sign * jnp.sin(angle)[None, :, :, None]
    real_part = values[:, 0]
    imag_part = values[:, 1]
    return jnp.stack(
        [real_part * cosine - imag_part * sine, real_part * sine + imag_part * cosine], 1
    )


def spectrum(signal):
    batch, half, width = signal.shape
    length = 2 * half
    outer_angle, inner_angle, twist_angle = angle_tables(length)
    outer_size = outer_angle.shape[0]
    inner_size = inner_angle.shape[0]
    folded = signal.reshape(batch, outer_size // 2, inner_size, width)
    used = outer_angle[:, : outer_size // 2]
    outer_table = jnp.stack([jnp.cos(used), -jnp.sin(used)])
    first = jnp.einsum("rka,pabc->prkbc", outer_table, folded, precision=precise)
    turned = twisted(first, twist_angle, -1.0)
    return jnp.einsum(
        "prkbc,rsbm->pskmc", turned, complex_table(inner_angle, -1.0), precision=precise
    )


def inverse(spec):
    batch, parts, outer_size, inner_size, width = spec.shape
    length = outer_size * inner_size
    outer_angle, inner_angle, twist_angle = angle_tables(length)
    back = jnp.einsum("pskmc,stmb->ptkbc", spec, complex_table(inner_angle, 1.0), precision=precise)
    turned = twisted(back, twist_angle, 1.0)
    used = outer_angle[: outer_size // 2]
    outer_table = jnp.stack([jnp.cos(used), -jnp.sin(used)])
    result = jnp.einsum("rak,prkbc->pabc", outer_table, turned, precision=precise)
    return (result / length).reshape(batch, length // 2, width)


def long_conv(channels, filter_spec, skip_gain, adjoint):
    signal = channels.astype(jnp.float32)
    spec = spectrum(signal)
    sig_real = spec[:, 0]
    sig_imag = spec[:, 1]
    filt_real = filter_spec[:, 0]
    filt_imag = filter_spec[:, 1]
    if adjoint:
        prod_real = sig_real * filt_real + sig_imag * filt_imag
        prod_imag = sig_imag * filt_real - sig_real * filt_imag
    else:
        prod_real = sig_real * filt_real - sig_imag * filt_imag
        prod_imag = sig_real * filt_imag + sig_imag * filt_real
    return (inverse(jnp.stack([prod_real, prod_imag], 1)) + skip_gain * signal).astype(jnp.bfloat16)


def depthwise(signal, filters):
    return lax.conv_general_dilated(
        signal,
        filters[:, None, :],
        (1,),
        "VALID",
        dimension_numbers=("NWC", "WIO", "NWC"),
        feature_group_count=signal.shape[2],
        preferred_element_type=jnp.float32,
    )


def to_channels(values):
    return lax.all_to_all(values, "ctx", split_axis=2, concat_axis=1, tiled=True)


def to_tokens(values):
    return lax.all_to_all(values, "ctx", split_axis=1, concat_axis=2, tiled=True)


def body(tokens, sub_pos, sub_base, embed, norm_gain, fir_taps, long_filter, skip_gain, cotangent):
    tok_rows = tokens.shape[0]
    width = embed.shape[1]
    reach = fir_taps.shape[1] - 1
    path_size = lax.axis_size("path")
    points = PATH_DEV * path_size
    in_block = jnp.arange(8, dtype=jnp.int32)[None, :] == (sub_pos % 8)[:, None]
    base_ids = jnp.where(in_block, sub_base[:, None], tokens.reshape(-1, 8)).reshape(-1)
    emb_tok = jnp.take(embed, tokens, axis=0).astype(jnp.float32)
    emb_base = jnp.take(embed, base_ids, axis=0).astype(jnp.float32)
    difference = emb_tok - emb_base
    first_point = lax.axis_index("path") * PATH_DEV
    alphas = (
        (first_point + jnp.arange(PATH_DEV, dtype=jnp.int32)).astype(jnp.float32) + 0.5
    ) / points
    inputs = emb_base[None] + alphas[:, None, None] * difference[None]
    inv_rms = lax.rsqrt(jnp.mean(inputs * inputs, -1, keepdims=True) + 1e-06)
    normed = (inputs * inv_rms * norm_gain).astype(jnp.bfloat16)
    earlier = from_behind(normed[:, tok_rows - reach :], "ctx", 1)
    extended = jnp.concatenate([earlier, normed], 1)
    flipped = fir_taps[:, ::-1, :]
    q_feat = depthwise(extended, flipped[0])
    k_feat = depthwise(extended, flipped[1])
    v_feat = depthwise(extended, flipped[2])
    gated = (k_feat * v_feat).astype(jnp.bfloat16)
    upstream = cotangent.astype(jnp.float32)[None]
    grad_y = (upstream * q_feat).astype(jnp.bfloat16)
    filter_spec = spectrum(long_filter[None])
    conv_out = to_tokens(long_conv(to_channels(gated), filter_spec, skip_gain, False))
    grad_z = to_tokens(long_conv(to_channels(grad_y), filter_spec, skip_gain, True))
    grad_z32 = grad_z.astype(jnp.float32)
    grad_q = (upstream * conv_out.astype(jnp.float32)).astype(jnp.bfloat16)
    grad_k = (grad_z32 * v_feat).astype(jnp.bfloat16)
    grad_v = (grad_z32 * k_feat).astype(jnp.bfloat16)
    grads = (grad_q, grad_k, grad_v)
    heads = jnp.stack([grad_q[:, :reach], grad_k[:, :reach], grad_v[:, :reach]])
    later = from_behind(heads, "ctx", -1)
    grad_norm = sum(
        (
            depthwise(jnp.concatenate([grads[index], later[index]], 1), fir_taps[index])
            for index in range(3)
        )
    )
    scaled = norm_gain * grad_norm
    grad_in = inv_rms * scaled - inputs * inv_rms**3 * jnp.mean(inputs * scaled, -1, keepdims=True)
    summed = lax.psum_scatter(
        jnp.sum(grad_in, 0).astype(jnp.bfloat16), "path", scatter_dimension=1, tiled=True
    ).astype(jnp.float32)
    path_grad = summed / points
    share = width // path_size
    columns = lax.dynamic_slice_in_dim(difference, lax.axis_index("path") * share, share, 1)
    return (path_grad, columns * path_grad)


def solution(mesh):
    return jax.shard_map(
        body,
        mesh=mesh,
        in_specs=(
            P("ctx"),
            P("ctx"),
            P("ctx"),
            P(),
            P(),
            P(),
            P(None, "ctx"),
            P("ctx"),
            P("ctx", None),
        ),
        out_specs=(P("ctx", "path"), P("ctx", "path")),
        check_vma=False,
    )
```

profile of v0, /device:TPU:1, one launch (start us, length us, event | category | flops | bytes accessed | tf_op | source)
XLA Modules:
  0.0 581.1 jit_solution(8248613599338435576)
XLA Ops:
  10.4 4.9 gather_fusion
  15.3 6.3 %gather_fusion.1 = bf16[128,4096]{1,0:T(8,128)(2,1)} fusion(bf16[512,4096]{1,0:T(8,128)(2,1)} %param.14, s32[1024]{0:T(1024)S(1)} %pad_clamp_fusion), kind=kCustom, calls=%fused_computation.1.clone | custom fusion | bytes 2097664 | tf_op jit(solution)/shard_map/jit(_take)/gather | solution.py:130
  28.2 4.2 collective-permute-start
  35.8 9.5 %slice.109 = bf16[1,3,4096]{2,1,0:T(4,128)(2,1)} reverse(bf16[1,3,4096]{2,1,0:T(4,128)(2,1)S(1)} %get-tuple-element.38), dimensions={1} | reverse | bytes 49152 | tf_op jit(solution)/shard_map/slice | solution.py:145
  45.3 9.5 %slice.107 = bf16[1,3,4096]{2,1,0:T(4,128)(2,1)} reverse(bf16[1,3,4096]{2,1,0:T(4,128)(2,1)S(1)} %get-tuple-element.36), dimensions={1} | reverse | bytes 49152 | tf_op jit(solution)/shard_map/slice | solution.py:144
  54.8 9.5 %slice.124 = bf16[1,3,4096]{2,1,0:T(4,128)(2,1)} reverse(bf16[1,3,4096]{2,1,0:T(4,128)(2,1)S(1)} %get-tuple-element.37), dimensions={1} | reverse | bytes 49152 | tf_op jit(solution)/shard_map/slice | solution.py:143
  83.6 5.5 copy.169
  89.7 24.4 %reduce.3 = bf16[4096,128]{1,0:T(8,128)(2,1)} reduce(bf16[4096,1,128]{2,1,0:T(2,128)(2,1)} %bitcast.293, bf16[]{:T(256)} %broadcast.627), dimensions={1}, to_apply=%bitcast.262.reduce_sub_computation | reduce | bytes 2097154
  116.2 10.4 %all-to-all-start = ((bf16[32,2,8192]{2,1,0:T(2,128)(2,1)}), bf16[32,2,8192]{2,1,0:T(2,128)(2,1)}, u32[]{:S(2)}, u32[]{:S(2)}) async-start(bf16[32,2,8192]{2,1,0:T(2,128)(2,1)} %reshape.653), calls=%async_computation | async-start | bytes 2097152 | tf_op jit(solution)/shard_map/all_to_all | solution.py:115
  131.4 3.5 reshape.576
  135.0 3.1 slice.167
  142.8 17.0 %copy.315 = bf16[1,128,4096]{1,0,2:T(2,128)(2,1)} copy(bf16[1,128,4096]{1,2,0:T(8,128)(2,1)S(1)} %fusion.47) | data formatting | bytes 2097152 | tf_op jit(solution)/shard_map/convert_element_type | solution.py:148
  159.9 23.5 %reduce.4 = bf16[4096,128]{1,0:T(8,128)(2,1)S(1)} reduce(bf16[4096,1,128]{2,1,0:T(2,128)(2,1)} %bitcast.295, bf16[]{:T(256)} %broadcast.627), dimensions={1}, to_apply=%bitcast.282.reduce_sub_computation | reduce | bytes 2097154
  184.5 9.4 %all-to-all-start.2 = ((bf16[32,2,8192]{2,1,0:T(2,128)(2,1)}), bf16[32,2,8192]{2,1,0:T(2,128)(2,1)S(1)}, u32[]{:S(2)}, u32[]{:S(2)}) async-start(bf16[32,2,8192]{2,1,0:T(2,128)(2,1)} %reshape.649), calls=%async_computation.2 | async-start | bytes 2097152 | tf_op jit(solution)/shard_map/all_to_all | solution.py:115
  194.8 6.9 %convolution_bitcast_fusion.1 = f32[1,2,64,128,128]{4,2,1,3,0:T(8,128)} fusion(f32[32,128,128,1]{2,1,0,3:T(8,128)S(1)} %bitcast.284, f32[1,64,32]{1,2,0:T(8,128)S(1)} %get-tuple-element.49, f32[1,64,32]{1,2,0:T(8,128)S(1)} %get-tuple-element.48), kind=kOutput, calls=%fused_computation.61 | convolution fusion | flops 402657280 | bytes 10502144 | tf_op jit(solution)/shard_map/rka,pabc->prkbc/dot_general | solution.py:67
  201.8 4.3 reshape.654
  209.1 6.4 %convolution_bitcast_fusion.2 = f32[1,2,64,128,128]{4,2,1,3,0:T(8,128)} fusion(bf16[1,128,32,128]{3,2,1,0:T(8,128)(2,1)S(1)} %copy.238, f32[1,64,32]{1,2,0:T(8,128)} %copy-done.24, f32[1,64,32]{1,2,0:T(8,128)S(1)} %get-tuple-element.48), kind=kOutput, calls=%fused_computation.62 | convolution fusion | flops 402657280 | bytes 9453568 | tf_op jit(solution)/shard_map/rka,pabc->prkbc/dot_general | solution.py:67
  219.4 3.1 convolution_bitcast_fusion
  223.3 12.8 %multiply_subtract_fusion.6 = (f32[1,1,64,128,128]{4,2,1,3,0:T(8,128)}, f32[1,1,64,128,128]{4,2,1,3,0:T(8,128)}, f32[1,1,64,128,128]{4,2,1,3,0:T(8,128)}, f32[1,...) fusion(f32[1,2,64,128,128]{4,2,1,3,0:T(8,128)} %convolution_bitcast_fusion.2, ...), kind=kLoop, calls=%fused_computation.54 | loop fusion | flops 18874368 | bytes 50397184 | tf_op jit(solution)/shard_map/sub | solution.py:54
  236.1 4.1 maximum_bitcast_fusion.5
  240.2 12.2 %fusion.33 = f32[1,2,64,128,128]{4,3,2,1,0:T(8,128)S(1)} fusion(f32[2,64,128,128]{3,1,0,2:T(8,128)} %maximum_bitcast_fusion.5, f32[1,2,128,128]{2,3,0,1:T(8,128)S(1)} %get-tuple-element.40, f32[1,2,128,128]{2,3,0,1:T(8,128)S(1)} %get-tuple-element.41), kind=kOutput, calls=%fused_computation.58 | convolution fusion | flops 3221291008 | bytes 17039360 | tf_op jit(solution)/shard_map/prkbc,rsbm->pskmc/dot_general | solution.py:69
  252.4 10.1 %maximum_bitcast_fusion = (f32[2,64,128,128]{3,1,0,2:T(8,128)}, f32[2,64,128,128]{3,1,0,2:T(8,128)}) fusion(f32[1,1,64,128,128]{4,2,1,3,0:T(8,128)} %get-tuple-element.14, f32[1,1,64,128,128]{4,2,1,3,0:T(8,128)S(1)} %copy-done.9, f32[1,1,64,128,128]{4,2,1,3,0:T(8,128)} %get-tuple-element.29, f32[1,1,64,128,128]{4,2,1,3,0:T(8,128)} %get-tuple-element.30), kind=kLoop, calls=%fused_computation.2 | loop fusion | flops 4194304 | bytes 33554432 | tf_op jit(solution)/shard_map/reshape.21
  262.5 14.1 %fusion.27 = f32[1,2,64,128,128]{4,3,2,1,0:T(8,128)} fusion(f32[2,64,128,128]{3,1,0,2:T(8,128)} %get-tuple-element.58, f32[1,2,128,128]{2,3,0,1:T(8,128)S(1)} %get-tuple-element.40, f32[1,2,128,128]{2,3,0,1:T(8,128)S(1)} %get-tuple-element.41), kind=kOutput, calls=%fused_computation.56 | convolution fusion | flops 3221291008 | bytes 17039360 | tf_op jit(solution)/shard_map/prkbc,rsbm->pskmc/dot_general | solution.py:69
  276.6 13.9 %fusion.24 = f32[1,2,64,128,128]{4,3,2,1,0:T(8,128)} fusion(f32[2,64,128,128]{3,1,0,2:T(8,128)S(1)} %copy-done.2, f32[1,2,128,128]{2,3,0,1:T(8,128)S(1)} %get-tuple-element.40, f32[1,2,128,128]{2,3,0,1:T(8,128)S(1)} %get-tuple-element.41), kind=kOutput, calls=%fused_computation.55 | convolution fusion | flops 3221291008 | bytes 17039360 | tf_op jit(solution)/shard_map/prkbc,rsbm->pskmc/dot_general | solution.py:69
  290.5 11.8 %multiply_subtract_fusion.4 = (f32[1,1,64,128,128]{4,3,2,1,0:T(8,128)}, f32[1,1,64,128,128]{4,3,2,1,0:T(8,128)}, f32[1,1,64,128,128]{4,3,2,1,0:T(8,128)}, f32[1,1,64,128,128]{4,3,2,1,0:T(8,128)}) fusion(f32[1,2,64,128,128]{4,3,2,1,0:T(8,128)} %fusion.24, f32[1,2,64,128,128]{4,3,2,1,0:T(8,128)} %fusion.27, f32[1,2,64,128,128]{4,3,2,1,0:T(8,128)S(1)} %fusion.33), kind=kLoop, calls=%fused_computation.50 | loop fusion | flops 12582912 | bytes 41943040 | tf_op jit(solution)/shard_map/sub | solution.py:97
  302.4 7.0 %fusion.36 = f32[2,128,64,128]{3,1,2,0:T(8,128)S(1)} fusion(f32[1,1,64,128,128]{4,3,2,1,0:T(8,128)} %get-tuple-element.21, f32[1,1,64,128,128]{4,3,2,1,0:T(8,128)} %get-tuple-element.22, f32[1,2,128,128]{2,3,1,0:T(8,128)S(1)} %copy-done.31, f32[1,2,128,128]{2,3,1,0:T(8,128)S(1)} %copy-done.30), kind=kOutput, calls=%fused_computation.59 | convolution fusion | flops 3223388160 | bytes 17039360 | tf_op jit(solution)/shard_map/pskmc,stmb->ptkbc/dot_general | solution.py:78
  309.3 4.9 copy.312
  314.2 8.9 %fusion.30 = f32[2,128,64,128]{3,1,2,0:T(8,128)} fusion(f32[1,1,64,128,128]{4,3,2,1,0:T(8,128)} %get-tuple-element.8, f32[1,1,64,128,128]{4,3,2,1,0:T(8,128)} %get-tuple-element.7, f32[1,2,128,128]{2,3,1,0:T(8,128)S(1)} %copy-done.31, f32[1,2,128,128]{2,3,1,0:T(8,128)S(1)} %copy-done.30), kind=kOutput, calls=%fused_computation.57 | convolution fusion | flops 3223388160 | bytes 17039360 | tf_op jit(solution)/shard_map/pskmc,stmb->ptkbc/dot_general | solution.py:78
  323.1 8.3 %copy.313 = f32[2,128,64,128]{3,2,0,1:T(8,128)S(1)} copy(f32[2,128,64,128]{3,1,2,0:T(8,128)} %fusion.30) | data formatting | bytes 16777216 | tf_op jit(solution)/shard_map/pskmc,stmb->ptkbc/dot_general | solution.py:78
  331.4 6.8 %multiply_subtract_fusion.3 = (f32[1,1,64,128,128]{4,2,1,3,0:T(8,128)S(1)}, f32[1,1,64,128,128]{4,2,1,3,0:T(8,128)}, f32[1,1,64,128,128]{4,2,1,3,0:T(8,128)}, f32[1,1,64,128,128]{4,2,1,3,0:T(8,128)}) fusion(f32[1,2,64,128,128]{4,2,1,3,0:T(8,128)S(1)} %bitcast.286, f32[64,128]{0,1:T(8,128)S(1)} %copy-done.26, f32[64,128]{0,1:T(8,128)S(1)} %fusion.115, ...), kind=kLoop, calls=%fused_computation.48 | loop fusion | flops 12582912 | bytes 33619968 | tf_op jit(solution)/shard_map/sub | solution.py:54
  338.2 4.8 fusion.54
  353.2 16.7 %copy.314 = bf16[1,4096,128]{2,0,1:T(2,128)(2,1)S(1)} copy(bf16[1,4096,128]{2,1,0:T(8,128)(2,1)S(1)} %get-tuple-element.53) | data formatting | bytes 2097152 | tf_op jit(solution)/shard_map/convert_element_type | solution.py:99
  369.8 22.7 %reduce.5 = bf16[4096,128]{1,0:T(8,128)(2,1)S(1)} reduce(bf16[4096,1,128]{2,1,0:T(2,128)(2,1)S(1)} %bitcast.296, bf16[]{:T(256)} %broadcast.627), dimensions={1}, to_apply=%bitcast.281.reduce_sub_computation | reduce | bytes 2097154
  393.6 9.5 %all-to-all-start.3 = ((bf16[32,2,8192]{2,1,0:T(2,128)(2,1)}), bf16[32,2,8192]{2,1,0:T(2,128)(2,1)S(1)}, u32[]{:S(2)}, u32[]{:S(2)}) async-start(bf16[32,2,8192]{2,1,0:T(2,128)(2,1)} %reshape.651), calls=%async_computation.3 | async-start | bytes 2097152 | tf_op jit(solution)/shard_map/all_to_all | solution.py:119
  403.1 4.8 copy.198
  407.9 3.0 copy.200
  410.9 3.6 reshape.580
  417.9 3.5 reshape.578
  424.9 3.2 copy.316
  428.1 23.4 %reduce.6 = bf16[4096,128]{1,0:T(8,128)(2,1)} reduce(bf16[4096,1,128]{2,1,0:T(2,128)(2,1)S(1)} %bitcast.294, bf16[]{:T(256)} %broadcast.627), dimensions={1}, to_apply=%bitcast.283.reduce_sub_computation | reduce | bytes 2097154
  453.6 9.5 %all-to-all-start.1 = ((bf16[32,2,8192]{2,1,0:T(2,128)(2,1)}), bf16[32,2,8192]{2,1,0:T(2,128)(2,1)}, u32[]{:S(2)}, u32[]{:S(2)}) async-start(bf16[32,2,8192]{2,1,0:T(2,128)(2,1)} %reshape.655), calls=%async_computation.1 | async-start | bytes 2097152 | tf_op jit(solution)/shard_map/all_to_all | solution.py:119
  466.9 3.2 fusion.50
  471.5 5.9 %all-to-all-done.1 = bf16[32,2,8192]{2,1,0:T(2,128)(2,1)} async-done(((bf16[32,2,8192]{2,1,0:T(2,128)(2,1)}), bf16[32,2,8192]{2,1,0:T(2,128)(2,1)}, u32[]{:S(2)}, u32[]{:S(2)}) %all-to-all-start.1) | async-done | bytes 1048608 | tf_op jit(solution)/shard_map/all_to_all | solution.py:119
  477.4 4.3 reshape.656
  492.3 3.5 collective-permute-done.1
  500.3 3.8 copy.256
  536.5 3.7 reshape.574
  545.1 26.8 %reduce-scatter.2.cloned.1.call-done = bf16[128,1024]{1,0:T(8,128)(2,1)} async-done(((bf16[128,4096]{1,0:T(8,128)(2,1)}), bf16[128,1024]{1,0:T(8,128)(2,1)}) %reduce-scatter.2.cloned.1.call-update) | async-done | bytes 262160 | tf_op jit(solution)/shard_map/reduce_scatter | solution.py:167
  (215 shorter events, 133.9 us)
Async XLA Ops:
  7.2 187.6 %copy-start = (f32[4096,128]{1,0:T(8,128)S(1)}, f32[4096,128]{1,0:T(8,128)}, u32[]{:S(2)}) copy-start(f32[4096,128]{1,0:T(8,128)} %param.17) | copy-start | bytes 6291460
  10.3 13.9 %copy-start.41 = (pred[128]{0:T(512)(128)(4,1)}, pred[128]{0:T(512)(128)(4,1)S(1)}, u32[]{:S(2)}) copy-start(pred[128]{0:T(512)(128)(4,1)S(1)} %get-tuple-element.5) | copy-start | bytes 388
  10.3 13.9 %copy-start.43 = (pred[128]{0:T(512)(128)(4,1)}, pred[128]{0:T(512)(128)(4,1)S(1)}, u32[]{:S(2)}) copy-start(pred[128]{0:T(512)(128)(4,1)S(1)} %get-tuple-element.54) | copy-start | bytes 388
  15.3 9.0 %copy-start.3 = (bf16[128,4096]{1,0:T(8,128)(2,1)}, bf16[128,4096]{1,0:T(8,128)(2,1)S(1)}, u32[]{:S(2)}) copy-start(bf16[128,4096]{1,0:T(8,128)(2,1)S(1)} %gather_fusion) | copy-start | bytes 3145732
  15.3 9.0 %copy-start.39 = (f32[4096]{0:T(1024)S(1)}, f32[4096]{0:T(1024)}, u32[]{:S(2)}) copy-start(f32[4096]{0:T(1024)} %param.15) | copy-start | bytes 49156
  21.6 2.6 copy-start.5
  24.3 2.2 copy-start.45
  24.3 9.2 %copy-start.32 = (bf16[3,3,4096]{2,1,0:T(4,128)(2,1)S(1)}, bf16[3,3,4096]{2,1,0:T(4,128)(2,1)}, u32[]{:S(2)}) copy-start(bf16[3,3,4096]{2,1,0:T(4,128)(2,1)} %param.16) | copy-start | bytes 221188
  28.2 37.8 %collective-permute-start = (bf16[1,2,4096]{2,1,0:T(2,128)(2,1)}, bf16[1,2,4096]{2,1,0:T(2,128)(2,1)S(1)}, u32[]{:S(2)}, u32[]{:S(2)}) collective-permute-start(bf16[1,2,4096]{2,1,0:T(2,128)(2,1)} %slice.151), channel_id=1, source_target_pairs={{0,1},{1,2},{2,3},{3,4},{4,5},{5,6},{6,7},{7,8},{8,9},{9,10},{10,1... | collective-permute-start | bytes 49160 | tf_op jit(solution)/shard_map/ppermute | solution.py:13
  32.4 36.5 %copy-start.27 = (f32[64,64]{0,1:T(8,128)}, f32[64,64]{0,1:T(8,128)S(1)}, u32[]{:S(2)}) copy-start(f32[64,64]{0,1:T(8,128)S(1)} %fusion.113) | copy-start | bytes 49156
  34.2 160.5 %copy-start.24 = (f32[1,64,32]{1,2,0:T(8,128)}, f32[1,64,32]{1,2,0:T(8,128)S(1)}, u32[]{:S(2)}) copy-start(f32[1,64,32]{1,2,0:T(8,128)S(1)} %get-tuple-element.49) | copy-start | bytes 24580
  65.9 75.1 %copy-start.11 = (bf16[128,4096]{0,1:T(8,128)(2,1)}, bf16[128,4096]{0,1:T(8,128)(2,1)S(1)}, u32[]{:S(2)}) copy-start(bf16[128,4096]{0,1:T(8,128)(2,1)S(1)} %copy.162) | copy-start | bytes 3145732
  68.8 5.0 copy-start.49
  71.7 2.1 copy-start.38
  74.5 2.2 copy-start.17
  114.1 12.6 %copy-start.36 = (bf16[1,3,4096]{2,1,0:T(4,128)(2,1)S(1)}, bf16[1,3,4096]{2,1,0:T(4,128)(2,1)}, u32[]{:S(2)}) copy-start(bf16[1,3,4096]{2,1,0:T(4,128)(2,1)} %slice.124) | copy-start | bytes 73732
  116.2 68.3 %all-to-all-start = ((bf16[32,2,8192]{2,1,0:T(2,128)(2,1)}), bf16[32,2,8192]{2,1,0:T(2,128)(2,1)}, u32[]{:S(2)}, u32[]{:S(2)}) async-start(bf16[32,2,8192]{2,1,0:T(2,128)(2,1)} %reshape.653), calls=%async_computation | async-start | bytes 2097152 | tf_op jit(solution)/shard_map/all_to_all | solution.py:115
  184.5 32.7 %all-to-all-start.2 = ((bf16[32,2,8192]{2,1,0:T(2,128)(2,1)}), bf16[32,2,8192]{2,1,0:T(2,128)(2,1)S(1)}, u32[]{:S(2)}, u32[]{:S(2)}) async-start(bf16[32,2,8192]{2,1,0:T(2,128)(2,1)} %reshape.649), calls=%async_computation.2 | async-start | bytes 2097152 | tf_op jit(solution)/shard_map/all_to_all | solution.py:115
  194.8 6.9 %copy-start.28 = (f32[64,64]{0,1:T(8,128)S(1)}, f32[64,64]{0,1:T(8,128)}, u32[]{:S(2)}) copy-start(f32[64,64]{0,1:T(8,128)} %copy-done.27) | copy-start | bytes 49156
  240.2 12.2 %copy-start.9 = (f32[1,1,64,128,128]{4,2,1,3,0:T(8,128)S(1)}, f32[1,1,64,128,128]{4,2,1,3,0:T(8,128)}, u32[]{:S(2)}) copy-start(f32[1,1,64,128,128]{4,2,1,3,0:T(8,128)} %get-tuple-element.13) | copy-start | bytes 12582916
  262.5 14.1 %copy-start.2 = (f32[2,64,128,128]{3,1,0,2:T(8,128)S(1)}, f32[2,64,128,128]{3,1,0,2:T(8,128)}, u32[]{:S(2)}) copy-start(f32[2,64,128,128]{3,1,0,2:T(8,128)} %get-tuple-element.57) | copy-start | bytes 25165828
  290.5 11.8 %copy-start.30 = (f32[1,2,128,128]{2,3,1,0:T(8,128)S(1)}, f32[1,2,128,128]{2,3,1,0:T(8,128)}, u32[]{:S(2)}) copy-start(f32[1,2,128,128]{2,3,1,0:T(8,128)} %get-tuple-element.39) | copy-start | bytes 393220
  290.5 11.8 %copy-start.31 = (f32[1,2,128,128]{2,3,1,0:T(8,128)S(1)}, f32[1,2,128,128]{2,3,1,0:T(8,128)}, u32[]{:S(2)}) copy-start(f32[1,2,128,128]{2,3,1,0:T(8,128)} %get-tuple-element.42) | copy-start | bytes 393220
  323.1 8.3 %copy-start.26 = (f32[64,128]{0,1:T(8,128)S(1)}, f32[64,128]{0,1:T(8,128)}, u32[]{:S(2)}) copy-start(f32[64,128]{0,1:T(8,128)} %fusion.114) | copy-start | bytes 98308
  343.0 2.2 copy-start.10
  347.6 1.6 copy-start.15
  393.6 60.1 %all-to-all-start.3 = ((bf16[32,2,8192]{2,1,0:T(2,128)(2,1)}), bf16[32,2,8192]{2,1,0:T(2,128)(2,1)S(1)}, u32[]{:S(2)}, u32[]{:S(2)}) async-start(bf16[32,2,8192]{2,1,0:T(2,128)(2,1)} %reshape.651), calls=%async_computation.3 | async-start | bytes 2097152 | tf_op jit(solution)/shard_map/all_to_all | solution.py:119
  403.1 4.8 copy-start.18
  414.5 1.6 slice-start
  421.5 1.6 slice-start.1
  453.6 23.8 %all-to-all-start.1 = ((bf16[32,2,8192]{2,1,0:T(2,128)(2,1)}), bf16[32,2,8192]{2,1,0:T(2,128)(2,1)}, u32[]{:S(2)}, u32[]{:S(2)}) async-start(bf16[32,2,8192]{2,1,0:T(2,128)(2,1)} %reshape.655), calls=%async_computation.1 | async-start | bytes 2097152 | tf_op jit(solution)/shard_map/all_to_all | solution.py:119
  463.1 108.7 %reduce-scatter.2.cloned.1.call-start = ((), (), s32[]{:S(2)}) async-start(), calls=%async_computation.5 | async-start | bytes 1310720 | tf_op jit(solution)/shard_map/reduce_scatter | solution.py:167
  483.5 3.0 copy-start.12
  488.3 9.0 %copy-start.14 = (bf16[1,128,4096]{1,2,0:T(8,128)(2,1)S(1)}, bf16[1,128,4096]{1,2,0:T(8,128)(2,1)}, u32[]{:S(2)}) copy-start(bf16[1,128,4096]{1,2,0:T(8,128)(2,1)} %copy-done.13) | copy-start | bytes 3145732
  491.0 4.8 collective-permute-start.1
  527.8 2.4 copy-start.35
  527.8 2.4 copy-start.50
  530.2 1.2 copy-start.23
  531.5 1.2 copy-start.40
  536.5 3.7 copy-start.4
  536.5 3.7 copy-start.6
  536.5 3.7 copy-start.42
  536.5 3.7 copy-start.44
  540.2 2.5 copy-start.7
  540.2 2.6 copy-start.8
  540.2 2.6 copy-start.46
  540.3 2.6 copy-start.47
  542.8 31.2 %copy-start.1 = (f32[4096,128]{1,0:T(8,128)S(1)}, f32[4096,128]{1,0:T(8,128)}, u32[]{:S(2)}) copy-start(f32[4096,128]{1,0:T(8,128)} %param.17) | copy-start | bytes 6291460
  (12 other events, 12.7 us)
Sparse Core Ops, SparseCore 0:
  545.2 26.6 reduce-scatter.1
where the time goes:
time: 589 us; the launch traced here: 581 us
  local copies, waits for them, and re-layouts  221 us (38%)
  other arithmetic  179 us (30%)
  matrix products  86 us (15%)
  starting transfers between devices  44.2 us (8%)
  waiting for transfers between devices  36.3 us (6%)
  between operations  15.1 us (3%)
    unnamed x4, other arithmetic  94 us
    unnamed x123, local copies, waits for them, and re-layouts  46.4 us
    conv_general_dilated x23, local copies, waits for them, and re-layouts, depthwise(): lax.conv_general_dilated(signal, filters[:, None, :], (1,), 'VALID', dime...  42.3 us
    dot_general x3, matrix products, spectrum(): jnp.einsum('prkbc,rsbm->pskmc', turned, complex_table(inner_angle, -1.0),...  40.2 us
    reduce_scatter x1, waiting for transfers between devices, body(): lax.psum_scatter(jnp.sum(grad_in, 0).astype(jnp.bfloat16), 'path', scatte...  26.8 us
    convert_element_type x2, local copies, waits for them, and re-layouts, long_conv(): (inverse(jnp.stack([prod_real, prod_imag], 1)) + skip_gain * signal).asty...  19.8 us
    all_to_all x2, starting transfers between devices, to_channels(): lax.all_to_all(values, 'ctx', split_axis=2, concat_axis=1, tiled=True)  19.8 us
    sub x2, other arithmetic, twisted(): real_part * cosine - imag_part * sine  19.6 us
  transfers between devices with their start and end apart: 7, of which 3 were waited for; matrix products, arithmetic and copies ran while one was open for 29% of the time, Pallas kernels for 0%

commit v1 on v0

--- a/solution.py
+++ b/solution.py
@@ -112,7 +112,10 @@
 
 
 def to_channels(values):
-    return lax.all_to_all(values, "ctx", split_axis=2, concat_axis=1, tiled=True)
+    return jnp.concatenate(
+        lax.all_to_all(jnp.stack(jnp.split(values, lax.axis_size("ctx"), axis=2)), "ctx", 0, 0),
+        axis=1,
+    )
 
 
 def to_tokens(values):

time: 589 us -> 544 us (0.924)
  other arithmetic: 179 us -> 128 us
    unnamed x4 -> x2, other arithmetic: 94 us -> 44.8 us
    convert_element_type x4 -> x66, local copies, waits for them, and re-layouts: 12.4 us -> 40.9 us  [body(): gated = (k_feat * v_feat).astype(jnp.bfloat16)]
    unnamed x123 -> x167, local copies, waits for them, and re-layouts: 46.4 us -> 72.1 us
    convert_element_type x4 -> x0, local copies, waits for them, and re-layouts: 21.3 us -> none  [the longest x1 17 us: body(): grad_y = (upstream * q_feat).astype(jnp.bfloat16)]
    conv_general_dilated x23 -> x14, local copies, waits for them, and re-layouts: 42.3 us -> 25.7 us  [depthwise(): lax.conv_general_dilated(signal, filters[:, None, :], (1,), 'VALID', dime...]
    convert_element_type x2, local copies, waits for them, and re-layouts: 19.8 us -> 33.3 us  [long_conv(): (inverse(jnp.stack([prod_real, prod_imag], 1)) + skip_gain * signal).asty...]
    slice x1, local copies, waits for them, and re-layouts: 9.48 us -> 0.81 us  [body(): v_feat = depthwise(extended, flipped[2])]
    slice x1, local copies, waits for them, and re-layouts: 9.48 us -> 0.84 us  [body(): k_feat = depthwise(extended, flipped[1])]
  transfers between devices with their start and end apart: 7 -> 7, of which waited for: 3 -> 3; matrix products, arithmetic and copies ran while one was open for 29% -> 33% of each run, Pallas kernels for 0% -> 0%
where the time goes in v1:
time: 544 us; the launch traced here: 533 us
  local copies, waits for them, and re-layouts  223 us (41%)
  other arithmetic  128 us (24%)
  matrix products  86.5 us (16%)
  starting transfers between devices  44.7 us (8%)
  waiting for transfers between devices  35.5 us (7%)
  between operations  15.5 us (3%)
    unnamed x167, local copies, waits for them, and re-layouts  72.1 us
    unnamed x2, other arithmetic  44.8 us
    convert_element_type x66, local copies, waits for them, and re-layouts, body(): gated = (k_feat * v_feat).astype(jnp.bfloat16)  40.9 us
    dot_general x3, matrix products, spectrum(): jnp.einsum('prkbc,rsbm->pskmc', turned, complex_table(inner_angle, -1.0),...  40 us
    convert_element_type x2, local copies, waits for them, and re-layouts, long_conv(): (inverse(jnp.stack([prod_real, prod_imag], 1)) + skip_gain * signal).asty...  33.3 us
    reduce_scatter x1, waiting for transfers between devices, body(): lax.psum_scatter(jnp.sum(grad_in, 0).astype(jnp.bfloat16), 'path', scatte...  26.7 us
    conv_general_dilated x14, local copies, waits for them, and re-layouts, depthwise(): lax.conv_general_dilated(signal, filters[:, None, :], (1,), 'VALID', dime...  25.7 us
    all_to_all x2, starting transfers between devices, to_channels(): lax.all_to_all(jnp.stack(jnp.split(values, lax.axis_size('ctx'), axis=2))...  19.8 us
  transfers between devices with their start and end apart: 7, of which 3 were waited for; matrix products, arithmetic and copies ran while one was open for 33% of the time, Pallas kernels for 0%

profile of v1, /device:TPU:1, one launch (start us, length us, event | category | flops | bytes accessed | tf_op | source)
XLA Modules:
  0.0 533.4 jit_solution(10372606073273615850)
XLA Ops:
  10.3 4.9 gather_fusion
  15.3 6.4 %gather_fusion.1 = bf16[128,4096]{1,0:T(8,128)(2,1)} fusion(bf16[512,4096]{1,0:T(8,128)(2,1)} %param.14, s32[1024]{0:T(1024)S(1)} %get-tuple-element.89), kind=kCustom, calls=%fused_computation.1.clone | custom fusion | bytes 2097664 | tf_op jit(solution)/shard_map/jit(_take)/gather | solution.py:133
  24.3 2.2 fusion.82
  27.6 4.2 collective-permute-start
  34.4 9.4 %slice.124 = bf16[1,3,4096]{2,1,0:T(4,128)(2,1)} reverse(bf16[1,3,4096]{2,1,0:T(4,128)(2,1)S(1)} %get-tuple-element.69), dimensions={1} | reverse | bytes 49152 | tf_op jit(solution)/shard_map/slice | solution.py:146
  52.3 2.1 multiply_convert_fusion
  57.0 3.0 copy.4142
  60.0 3.6 reshape.642
  85.0 10.1 %all-to-all-start.2 = ((bf16[32,1,128,128]{3,2,1,0:T(8,128)(2,1)}), bf16[32,1,128,128]{3,2,1,0:T(8,128)(2,1)S(1)}, u32[]{:S(2)}, u32[]{:S(2)}) async-start(bf16[32,1,128,128]{3,2,1,0:T(8,128)(2,1)} %constant_dynamic-update-slice_fusion.32), calls=%async_computation.2 | async-start | bytes 2097152 | tf_op jit(solution)/shard_map/all_to_all | solution.py:116
  174.4 9.8 %all-to-all-start = ((bf16[32,1,128,128]{3,2,1,0:T(8,128)(2,1)}), bf16[32,1,128,128]{3,2,1,0:T(8,128)(2,1)}, u32[]{:S(2)}, u32[]{:S(2)}) async-start(bf16[32,1,128,128]{3,2,1,0:T(8,128)(2,1)} %constant_dynamic-update-slice_fusion), calls=%async_computation | async-start | bytes 2097152 | tf_op jit(solution)/shard_map/all_to_all | solution.py:116
  189.4 6.9 %convolution_bitcast_fusion.1 = f32[1,2,64,128,128]{4,2,1,3,0:T(8,128)} fusion(f32[32,128,128,1]{2,1,0,3:T(8,128)S(1)} %bitcast.530, f32[1,64,32]{1,2,0:T(8,128)S(1)} %get-tuple-element.81, f32[1,64,32]{1,2,0:T(8,128)S(1)} %get-tuple-element.80), kind=kOutput, calls=%fused_computation.61 | convolution fusion | flops 402657280 | bytes 10502144 | tf_op jit(solution)/shard_map/rka,pabc->prkbc/dot_general | solution.py:67
  196.2 5.7 %convolution_bitcast_fusion = f32[1,2,64,128,128]{4,2,1,3,0:T(8,128)} fusion(bf16[32,1,128,128]{3,2,1,0:T(8,128)(2,1)S(1)} %all-to-all-done.2, f32[1,64,32]{1,2,0:T(8,128)S(1)} %get-tuple-element.81, f32[1,64,32]{1,2,0:T(8,128)S(1)} %get-tuple-element.80), kind=kOutput, calls=%fused_computation.60 | convolution fusion | flops 402657280 | bytes 9453568 | tf_op jit(solution)/shard_map/rka,pabc->prkbc/dot_general | solution.py:67
  201.9 3.8 convolution_bitcast_fusion.2
  205.7 10.9 %multiply_subtract_fusion.6 = (f32[1,1,64,128,128]{4,2,1,3,0:T(8,128)}, f32[1,1,64,128,128]{4,2,1,3,0:T(8,128)}, f32[1,1,64,128,128]{4,2,1,3,0:T(8,128)S(1)}, f3...) fusion(f32[1,2,64,128,128]{4,2,1,3,0:T(8,128)S(1)} %convolution_bitcast_fusion, ...), kind=kLoop, calls=%fused_computation.54 | loop fusion | flops 18874368 | bytes 50397184 | tf_op jit(solution)/shard_map/sub | solution.py:54
  216.7 8.4 %maximum_bitcast_fusion.5 = f32[2,64,128,128]{3,1,0,2:T(8,128)} fusion(f32[1,1,64,128,128]{4,2,1,3,0:T(8,128)} %get-tuple-element.63, f32[1,1,64,128,128]{4,2,1,3,0:T(8,128)} %get-tuple-element.64), kind=kLoop, calls=%fused_computation.9 | loop fusion | flops 2097152 | bytes 16777216 | tf_op jit(solution)/shard_map/reshape.39
  225.1 4.1 maximum_bitcast_fusion.1
  229.2 12.2 %fusion.33 = f32[1,2,64,128,128]{4,3,2,1,0:T(8,128)S(1)} fusion(f32[2,64,128,128]{3,1,0,2:T(8,128)} %maximum_bitcast_fusion.5, f32[1,2,128,128]{2,3,0,1:T(8,128)S(1)} %get-tuple-element.72, f32[1,2,128,128]{2,3,0,1:T(8,128)S(1)} %get-tuple-element.73), kind=kOutput, calls=%fused_computation.58 | convolution fusion | flops 3221291008 | bytes 17039360 | tf_op jit(solution)/shard_map/prkbc,rsbm->pskmc/dot_general | solution.py:69
  241.5 13.8 %fusion.27 = f32[1,2,64,128,128]{4,3,2,1,0:T(8,128)} fusion(f32[2,64,128,128]{3,1,0,2:T(8,128)S(1)} %copy-done.2, f32[1,2,128,128]{2,3,0,1:T(8,128)S(1)} %get-tuple-element.72, f32[1,2,128,128]{2,3,0,1:T(8,128)S(1)} %get-tuple-element.73), kind=kOutput, calls=%fused_computation.56 | convolution fusion | flops 3221291008 | bytes 17039360 | tf_op jit(solution)/shard_map/prkbc,rsbm->pskmc/dot_general | solution.py:69
  255.2 6.7 %maximum_bitcast_fusion = f32[2,64,128,128]{3,1,0,2:T(8,128)} fusion(f32[1,1,64,128,128]{4,2,1,3,0:T(8,128)} %get-tuple-element.14, f32[1,1,64,128,128]{4,2,1,3,0:T(8,128)S(1)} %copy-done.10), kind=kLoop, calls=%fused_computation.2 | loop fusion | flops 2097152 | bytes 16777216 | tf_op jit(solution)/shard_map/reshape.23
  262.0 14.1 %fusion.24 = f32[1,2,64,128,128]{4,3,2,1,0:T(8,128)} fusion(f32[2,64,128,128]{3,1,0,2:T(8,128)} %maximum_bitcast_fusion, f32[1,2,128,128]{2,3,0,1:T(8,128)S(1)} %get-tuple-element.72, f32[1,2,128,128]{2,3,0,1:T(8,128)S(1)} %get-tuple-element.73), kind=kOutput, calls=%fused_computation.55 | convolution fusion | flops 3221291008 | bytes 17039360 | tf_op jit(solution)/shard_map/prkbc,rsbm->pskmc/dot_general | solution.py:69
  276.0 11.9 %multiply_subtract_fusion.4 = (f32[1,1,64,128,128]{4,3,2,1,0:T(8,128)}, f32[1,1,64,128,128]{4,3,2,1,0:T(8,128)}, f32[1,1,64,128,128]{4,3,2,1,0:T(8,128)}, f32[1,1,64,128,128]{4,3,2,1,0:T(8,128)}) fusion(f32[1,2,64,128,128]{4,3,2,1,0:T(8,128)} %fusion.24, f32[1,2,64,128,128]{4,3,2,1,0:T(8,128)} %fusion.27, f32[1,2,64,128,128]{4,3,2,1,0:T(8,128)S(1)} %fusion.33), kind=kLoop, calls=%fused_computation.50 | loop fusion | flops 12582912 | bytes 41943040 | tf_op jit(solution)/shard_map/sub | solution.py:97
  287.9 6.9 %fusion.36 = f32[2,128,64,128]{3,1,2,0:T(8,128)S(1)} fusion(f32[1,2,128,128]{2,3,0,1:T(8,128)S(1)} %copy-done.32, f32[1,2,128,128]{2,3,0,1:T(8,128)S(1)} %copy-done.31, f32[1,1,64,128,128]{4,3,2,1,0:T(8,128)} %get-tuple-element.21, f32[1,1,64,128,128]{4,3,2,1,0:T(8,128)} %get-tuple-element.22), kind=kOutput, calls=%fused_computation.59 | convolution fusion | flops 3223388160 | bytes 17039360 | tf_op jit(solution)/shard_map/pskmc,stmb->ptkbc/dot_general | solution.py:78
  294.8 4.9 copy.4265
  299.7 8.9 %fusion.30 = f32[2,128,64,128]{3,1,2,0:T(8,128)} fusion(f32[1,2,128,128]{2,3,0,1:T(8,128)S(1)} %copy-done.32, f32[1,2,128,128]{2,3,0,1:T(8,128)S(1)} %copy-done.31, f32[1,1,64,128,128]{4,3,2,1,0:T(8,128)} %get-tuple-element.8, f32[1,1,64,128,128]{4,3,2,1,0:T(8,128)} %get-tuple-element.7), kind=kOutput, calls=%fused_computation.57 | convolution fusion | flops 3223388160 | bytes 17039360 | tf_op jit(solution)/shard_map/pskmc,stmb->ptkbc/dot_general | solution.py:78
  308.6 8.3 %copy.4266 = f32[2,128,64,128]{3,2,0,1:T(8,128)S(1)} copy(f32[2,128,64,128]{3,1,2,0:T(8,128)} %fusion.30) | data formatting | bytes 16777216 | tf_op jit(solution)/shard_map/pskmc,stmb->ptkbc/dot_general | solution.py:78
  316.9 6.8 %multiply_subtract_fusion.3 = (f32[1,1,64,128,128]{4,2,1,3,0:T(8,128)S(1)}, f32[1,1,64,128,128]{4,2,1,3,0:T(8,128)}, f32[1,1,64,128,128]{4,2,1,3,0:T(8,128)}, f32[1,1,64,128,128]{4,2,1,3,0:T(8,128)}) fusion(f32[1,2,64,128,128]{4,2,1,3,0:T(8,128)S(1)} %bitcast.532, f32[64,128]{0,1:T(8,128)S(1)} %copy-done.26, f32[64,128]{0,1:T(8,128)S(1)} %get-tuple-element.92, ...), kind=kLoop, calls=%fused_computation.48 | loop fusion | flops 12582912 | bytes 33619968 | tf_op jit(solution)/shard_map/sub | solution.py:54
  323.7 4.8 fusion.62
  330.7 2.4 fusion.63
  334.4 2.8 fusion.59
  337.2 16.7 %copy.4268 = bf16[1,4096,128]{2,0,1:T(2,128)(2,1)S(1)} copy(bf16[1,4096,128]{2,1,0:T(8,128)(2,1)S(1)} %get-tuple-element.84) | data formatting | bytes 2097152 | tf_op jit(solution)/shard_map/convert_element_type | solution.py:99
  354.4 22.4 %reduce.4 = bf16[4096,128]{1,0:T(8,128)(2,1)S(1)} reduce(bf16[4096,1,128]{2,1,0:T(2,128)(2,1)S(1)} %bitcast.536, bf16[]{:T(256)} %broadcast.617), dimensions={1}, to_apply=%bitcast.529.reduce_sub_computation | reduce | bytes 2097154
  377.9 9.7 %all-to-all-start.1 = ((bf16[32,2,8192]{2,1,0:T(2,128)(2,1)}), bf16[32,2,8192]{2,1,0:T(2,128)(2,1)}, u32[]{:S(2)}, u32[]{:S(2)}) async-start(bf16[32,2,8192]{2,1,0:T(2,128)(2,1)} %reshape.744), calls=%async_computation.1 | async-start | bytes 2097152 | tf_op jit(solution)/shard_map/all_to_all | solution.py:122
  387.6 4.8 copy.4151
  392.4 3.0 copy.4152
  395.4 3.6 reshape.646
  399.1 3.6 reshape.644
  402.7 16.7 %copy.4267 = bf16[1,4096,128]{2,0,1:T(2,128)(2,1)S(1)} copy(bf16[1,4096,128]{2,1,0:T(8,128)(2,1)S(1)} %copy-done.20) | data formatting | bytes 2097152 | tf_op jit(solution)/shard_map/convert_element_type | solution.py:99
  419.4 22.4 %reduce.3 = bf16[4096,128]{1,0:T(8,128)(2,1)S(1)} reduce(bf16[4096,1,128]{2,1,0:T(2,128)(2,1)S(1)} %bitcast.537, bf16[]{:T(256)} %broadcast.617), dimensions={1}, to_apply=%bitcast.528.reduce_sub_computation | reduce | bytes 2097154
  442.9 9.4 %all-to-all-start.3 = ((bf16[32,2,8192]{2,1,0:T(2,128)(2,1)}), bf16[32,2,8192]{2,1,0:T(2,128)(2,1)S(1)}, u32[]{:S(2)}, u32[]{:S(2)}) async-start(bf16[32,2,8192]{2,1,0:T(2,128)(2,1)} %reshape.742), calls=%async_computation.3 | async-start | bytes 2097152 | tf_op jit(solution)/shard_map/all_to_all | solution.py:122
  452.3 4.3 reshape.745
  461.1 5.5 %all-to-all-done.3 = bf16[32,2,8192]{2,1,0:T(2,128)(2,1)S(1)} async-done(((bf16[32,2,8192]{2,1,0:T(2,128)(2,1)}), bf16[32,2,8192]{2,1,0:T(2,128)(2,1)S(1)}, u32[]{:S(2)}, u32[]{:S(2)}) %all-to-all-start.3) | async-done | bytes 1048608 | tf_op jit(solution)/shard_map/all_to_all | solution.py:122
  472.9 3.3 collective-permute-done.1
  485.6 3.0 copy.4159
  488.6 3.7 reshape.640
  492.4 2.5 fusion.61
  494.9 2.3 fusion.83
  497.2 26.7 %reduce-scatter.2.cloned.1.call-done = bf16[128,1024]{1,0:T(8,128)(2,1)} async-done(((bf16[128,4096]{1,0:T(8,128)(2,1)}), bf16[128,1024]{1,0:T(8,128)(2,1)}) %reduce-scatter.2.cloned.1.call-update) | async-done | bytes 262160 | tf_op jit(solution)/shard_map/reduce_scatter | solution.py:170
  523.9 2.2 dynamic-slice_multiply_fusion
  (302 shorter events, 152.5 us)
Async XLA Ops:
  7.2 182.2 %copy-start = (f32[4096,128]{1,0:T(8,128)S(1)}, f32[4096,128]{1,0:T(8,128)}, u32[]{:S(2)}) copy-start(f32[4096,128]{1,0:T(8,128)} %param.17) | copy-start | bytes 6291460
  10.3 14.0 %copy-start.40 = (pred[128]{0:T(512)(128)(4,1)}, pred[128]{0:T(512)(128)(4,1)S(1)}, u32[]{:S(2)}) copy-start(pred[128]{0:T(512)(128)(4,1)S(1)} %get-tuple-element.5) | copy-start | bytes 388
  10.3 14.0 %copy-start.42 = (pred[128]{0:T(512)(128)(4,1)}, pred[128]{0:T(512)(128)(4,1)S(1)}, u32[]{:S(2)}) copy-start(pred[128]{0:T(512)(128)(4,1)S(1)} %get-tuple-element.86) | copy-start | bytes 388
  15.3 9.0 %copy-start.4 = (bf16[128,4096]{1,0:T(8,128)(2,1)}, bf16[128,4096]{1,0:T(8,128)(2,1)S(1)}, u32[]{:S(2)}) copy-start(bf16[128,4096]{1,0:T(8,128)(2,1)S(1)} %gather_fusion) | copy-start | bytes 3145732
  15.3 9.0 %copy-start.38 = (f32[4096]{0:T(1024)S(1)}, f32[4096]{0:T(1024)}, u32[]{:S(2)}) copy-start(f32[4096]{0:T(1024)} %param.15) | copy-start | bytes 49156
  21.7 2.7 copy-start.6
  24.3 2.2 copy-start.46
  24.3 8.4 %copy-start.33 = (bf16[3,3,4096]{2,1,0:T(4,128)(2,1)S(1)}, bf16[3,3,4096]{2,1,0:T(4,128)(2,1)}, u32[]{:S(2)}) copy-start(bf16[3,3,4096]{2,1,0:T(4,128)(2,1)} %param.16) | copy-start | bytes 221188
  27.6 17.9 %collective-permute-start = (bf16[1,2,4096]{2,1,0:T(2,128)(2,1)S(1)}, bf16[1,2,4096]{2,1,0:T(2,128)(2,1)S(1)}, u32[]{:S(2)}, u32[]{:S(2)}) collective-permute-start(bf16[1,2,4096]{2,1,0:T(2,128)(2,1)S(1)} %slice.214), channel_id=1, source_target_pairs={{0,1},{1,2},{2,3},{3,4},{4,5},{5,6},{6,7},{7,8},{8,9},{9,10},{10,1... | collective-permute-start | bytes 49160 | tf_op jit(solution)/shard_map/ppermute | solution.py:13
  31.8 1.6 copy-start.27
  48.6 2.8 copy-start.44
  52.3 2.1 copy-start.12
  54.5 1.6 copy-start.37
  60.0 3.6 copy-start.21
  85.0 89.3 %all-to-all-start.2 = ((bf16[32,1,128,128]{3,2,1,0:T(8,128)(2,1)}), bf16[32,1,128,128]{3,2,1,0:T(8,128)(2,1)S(1)}, u32[]{:S(2)}, u32[]{:S(2)}) async-start(bf16[32,1,128,128]{3,2,1,0:T(8,128)(2,1)} %constant_dynamic-update-slice_fusion.32), calls=%async_computation.2 | async-start | bytes 2097152 | tf_op jit(solution)/shard_map/all_to_all | solution.py:116
  134.5 32.8 %copy-start.29 = (bf16[1,136,128]{2,1,0:T(8,128)(2,1)S(1)}, bf16[1,136,128]{2,1,0:T(8,128)(2,1)}, u32[]{:S(2)}) copy-start(bf16[1,136,128]{2,1,0:T(8,128)(2,1)} %reshape.604) | copy-start | bytes 104452
  135.1 34.1 %copy-start.30 = (bf16[1,136,128]{2,1,0:T(8,128)(2,1)S(1)}, bf16[1,136,128]{2,1,0:T(8,128)(2,1)}, u32[]{:S(2)}) copy-start(bf16[1,136,128]{2,1,0:T(8,128)(2,1)} %reshape.608) | copy-start | bytes 104452
  174.4 27.6 %all-to-all-start = ((bf16[32,1,128,128]{3,2,1,0:T(8,128)(2,1)}), bf16[32,1,128,128]{3,2,1,0:T(8,128)(2,1)}, u32[]{:S(2)}, u32[]{:S(2)}) async-start(bf16[32,1,128,128]{3,2,1,0:T(8,128)(2,1)} %constant_dynamic-update-slice_fusion), calls=%async_computation | async-start | bytes 2097152 | tf_op jit(solution)/shard_map/all_to_all | solution.py:116
  201.9 3.8 copy-start.25
  201.9 3.8 copy-start.3
  229.2 12.2 %copy-start.2 = (f32[2,64,128,128]{3,1,0,2:T(8,128)S(1)}, f32[2,64,128,128]{3,1,0,2:T(8,128)}, u32[]{:S(2)}) copy-start(f32[2,64,128,128]{3,1,0,2:T(8,128)} %maximum_bitcast_fusion.1) | copy-start | bytes 25165828
  241.4 13.8 %copy-start.10 = (f32[1,1,64,128,128]{4,2,1,3,0:T(8,128)S(1)}, f32[1,1,64,128,128]{4,2,1,3,0:T(8,128)}, u32[]{:S(2)}) copy-start(f32[1,1,64,128,128]{4,2,1,3,0:T(8,128)} %get-tuple-element.13) | copy-start | bytes 12582916
  276.0 11.9 %copy-start.31 = (f32[1,2,128,128]{2,3,0,1:T(8,128)S(1)}, f32[1,2,128,128]{2,3,0,1:T(8,128)}, u32[]{:S(2)}) copy-start(f32[1,2,128,128]{2,3,0,1:T(8,128)} %get-tuple-element.71) | copy-start | bytes 393220
  276.0 11.9 %copy-start.32 = (f32[1,2,128,128]{2,3,0,1:T(8,128)S(1)}, f32[1,2,128,128]{2,3,0,1:T(8,128)}, u32[]{:S(2)}) copy-start(f32[1,2,128,128]{2,3,0,1:T(8,128)} %get-tuple-element.74) | copy-start | bytes 393220
  308.6 8.3 %copy-start.26 = (f32[64,128]{0,1:T(8,128)S(1)}, f32[64,128]{0,1:T(8,128)}, u32[]{:S(2)}) copy-start(f32[64,128]{0,1:T(8,128)} %fusion.117) | copy-start | bytes 98308
  316.9 6.8 %copy-start.28 = (f32[1,32,64]{2,1,0:T(8,128)S(1)}, f32[1,32,64]{2,1,0:T(8,128)}, u32[]{:S(2)}) copy-start(f32[1,32,64]{2,1,0:T(8,128)} %copy.4136) | copy-start | bytes 24580
  328.5 2.2 copy-start.11
  377.9 65.0 %all-to-all-start.1 = ((bf16[32,2,8192]{2,1,0:T(2,128)(2,1)}), bf16[32,2,8192]{2,1,0:T(2,128)(2,1)}, u32[]{:S(2)}, u32[]{:S(2)}) async-start(bf16[32,2,8192]{2,1,0:T(2,128)(2,1)} %reshape.744), calls=%async_computation.1 | async-start | bytes 2097152 | tf_op jit(solution)/shard_map/all_to_all | solution.py:122
  387.6 4.8 copy-start.13
  399.1 3.6 copy-start.20
  442.9 23.7 %all-to-all-start.3 = ((bf16[32,2,8192]{2,1,0:T(2,128)(2,1)}), bf16[32,2,8192]{2,1,0:T(2,128)(2,1)S(1)}, u32[]{:S(2)}, u32[]{:S(2)}) async-start(bf16[32,2,8192]{2,1,0:T(2,128)(2,1)} %reshape.742), calls=%async_computation.3 | async-start | bytes 2097152 | tf_op jit(solution)/shard_map/all_to_all | solution.py:122
  452.3 71.7 %reduce-scatter.2.cloned.1.call-start = ((), (), s32[]{:S(2)}) async-start(), calls=%async_computation.5 | async-start | bytes 1310720 | tf_op jit(solution)/shard_map/reduce_scatter | solution.py:170
  467.6 1.6 copy-start.14
  471.3 5.0 copy-start.15
  471.4 4.8 collective-permute-start.1
  476.8 1.6 copy-start.19
  478.9 1.5 copy-start.16
  481.7 1.4 copy-start.35
  483.1 1.4 copy-start.39
  488.6 3.7 copy-start.5
  488.6 3.7 copy-start.7
  488.6 3.7 copy-start.41
  488.6 3.7 copy-start.43
  492.4 2.5 copy-start.8
  492.4 2.6 copy-start.9
  492.4 2.6 copy-start.47
  492.4 2.6 copy-start.49
  494.9 31.2 %copy-start.1 = (f32[4096,128]{1,0:T(8,128)S(1)}, f32[4096,128]{1,0:T(8,128)}, u32[]{:S(2)}) copy-start(f32[4096,128]{1,0:T(8,128)} %param.17) | copy-start | bytes 6291460
  (9 other events, 10.2 us)
Sparse Core Ops, SparseCore 0:
  497.3 26.5 reduce-scatter.1
